TPU v7x, 256 devices: a whole 4x4x8 slice. The times are simulated.
256 devices in a mesh: gx: 2 (over core), gy: 4 (over x), gz: 32 (over z, y).
Axes of the slice: x: 4, y: 4, z: 8, core: 2. Of those that a mesh axis runs over, the one named last changes fastest.
Arguments:
- resid_x: float32 [6, 8, 32, 120, 512], P('gx', 'gy', 'gz'), may hold values from -6 to 6
- resid_y: float32 [4, 12, 32, 120, 512], P('gx', 'gy', 'gz'), may hold values from -6 to 6
- face_weights: float32 [4, 8, 32, 4, 120], P('gx', 'gy', 'gz'), may hold values from 0.25 to 0.75
- face_counts: int32 [4, 8, 32, 4], P('gx', 'gy', 'gz'), may hold values from 1 to 4, as said below
- neumann: bfloat16 [4, 8, 32, 480, 480], P('gx', 'gy', 'gz'), may hold values from -0.25 to 0.25
- schur: bfloat16 [4, 8, 32, 480, 480], P('gx', 'gy', 'gz'), may hold values from -0.25 to 0.25
- basis: bfloat16 [4, 8, 32, 480, 64], P('gx', 'gy', 'gz'), may hold values from -0.25 to 0.25
- coarse_map: int32 [4, 8, 32, 64], P('gx', 'gy', 'gz'), may hold values from 0 to 511
- column_inverse: float32 [2, 4, 512, 512], P('gx', 'gy', 'gz'), may hold values from -0.25 to 0.25
- column_basis: float32 [2, 4, 512, 512], P('gx', 'gy', 'gz'), may hold values from -0.25 to 0.25
- top_inverse: float32 [512, 512], replicated, may hold values from -0.09375 to 0.09375
Outputs:
- z_x: float32 [6, 8, 32, 120, 512], P('gx', 'gy', 'gz')
- z_y: float32 [4, 12, 32, 120, 512], P('gx', 'gy', 'gz')
- schur_image: bfloat16 [4, 8, 32, 480, 512], P('gx', 'gy', 'gz')
Inputs may be any that keep to these rules, and one draw needn't show every extreme that they name: `face_counts`: only the first 30 * count of a face's 120 dofs are live; about one face in eight has 4 live mesh faces. `coarse_map`: several local coarse dofs may share a column coarse dof.
All inputs are finite; a program needn't handle non-finite values.
Results may differ from a plain program's by a relative error of at most 0.0063.
Values sent between devices are 32-bit elements; how exact they have to be, the bound alone decides.
No kernel may reach another device: no remote copies, remote signals or barrier semaphores. Data moves between devices by JAX's collectives and lax.ppermute only.
A program may use at most 64 MiB of HBM per device.

v0:
```python
import jax
import jax.numpy as jnp
from jax import lax
from jax.sharding import PartitionSpec as P

BLK = 30


def with_halo(array, sides, width):
    for axis, dim in sides:
        size, length = (lax.axis_size(axis), array.shape[dim])
        up = [(i, (i + 1) % size) for i in range(size)]
        down = [(j, i) for i, j in up]
        last = lax.slice_in_dim(array, length - width, length, axis=dim)
        initial = lax.slice_in_dim(array, 0, width, axis=dim)
        before = lax.ppermute(last, axis, up)
        after = lax.ppermute(initial, axis, down)
        array = jnp.concatenate([before, array, after], axis=dim)
    return array


def assemble_x(copies):
    padded = with_halo(copies, (("gx", 0),), 1)
    return copies + jnp.stack([padded[0], jnp.zeros_like(padded[0]), padded[4]], 0)


def assemble_y(copies):
    padded = with_halo(copies, (("gy", 1),), 1)
    return copies + jnp.stack([padded[:, 0], jnp.zeros_like(padded[:, 0]), padded[:, 4]], 1)


def gather_faces(along_x, along_y):
    return jnp.stack([along_x[0:2], along_x[1:3], along_y[:, 0:2], along_y[:, 1:3]], 2)


def on_device(
    resid_x,
    resid_y,
    face_weights,
    face_counts,
    neumann,
    schur,
    basis,
    coarse_map,
    column_inverse,
    column_basis,
    top_inverse,
):
    high = lax.Precision.HIGHEST
    face_dofs = resid_x.shape[3]
    loads = resid_x.shape[4]
    inner = neumann.shape[3]
    coarse_local = basis.shape[4]
    column_size = column_inverse.shape[3]
    dof_index = jnp.arange(face_dofs, dtype=jnp.int32)
    live = (dof_index[None, None, None, :] < face_counts[:, :, 0, :, None] * BLK).astype(
        jnp.float32
    )
    scale = face_weights[:, :, 0] * live
    assembled_x = assemble_x(resid_x)[:, :, 0]
    assembled_y = assemble_y(resid_y)[:, :, 0]
    faces = gather_faces(assembled_x, assembled_y)
    upart = (faces * scale[..., None]).reshape(4, inner, loads).astype(jnp.bfloat16)
    neumann_flat = neumann.reshape(4, inner, inner)
    basis_flat = basis.reshape(4, inner, coarse_local)
    wpart = jnp.einsum("snk,skr->snr", neumann_flat, upart, preferred_element_type=jnp.float32)
    gpart = jnp.einsum("snc,snr->scr", basis_flat, upart, preferred_element_type=jnp.float32)
    targets = coarse_map.reshape(4 * coarse_local)
    onehot = (targets[:, None] == jnp.arange(column_size, dtype=jnp.int32)[None, :]).astype(
        jnp.float32
    )
    column_part = lax.dot_general(
        onehot, gpart.reshape(4 * coarse_local, loads), (((0,), (0,)), ((), ())), precision=high
    )
    column_res = lax.psum(column_part, "gz")
    inverse_rows = column_inverse[0, 0]
    basis_rows = column_basis[0, 0]
    row_count = inverse_rows.shape[0]
    row_start = lax.axis_index("gz") * row_count
    own_rows = lax.dynamic_slice_in_dim(column_res, row_start, row_count, 0)
    level_two = jnp.dot(inverse_rows, column_res, precision=high)
    top_part = lax.dot_general(basis_rows, own_rows, (((0,), (0,)), ((), ())), precision=high)
    column_top = lax.psum(top_part, "gz")
    top_res = lax.psum(column_top, ("gx", "gy"))
    level_three = jnp.dot(top_inverse, top_res, precision=high)
    value_rows = level_two + jnp.dot(basis_rows, level_three, precision=high)
    column_vals = lax.all_gather(value_rows, "gz", axis=0, tiled=True)
    coarse_vals = (
        jnp.dot(onehot, column_vals, precision=high)
        .reshape(4, coarse_local, loads)
        .astype(jnp.bfloat16)
    )
    ypart = wpart + jnp.einsum(
        "snc,scr->snr", basis_flat, coarse_vals, preferred_element_type=jnp.float32
    )
    contrib = ypart.reshape(2, 2, 4, face_dofs, loads) * scale[..., None]
    send_x = jnp.stack(
        [contrib[0, :, 0], contrib[0, :, 1] + contrib[1, :, 0], contrib[1, :, 1]], 0
    )[:, :, None]
    send_y = jnp.stack(
        [contrib[:, 0, 2], contrib[:, 0, 3] + contrib[:, 1, 2], contrib[:, 1, 3]], 1
    )[:, :, None]
    z_x = assemble_x(send_x)
    z_y = assemble_y(send_y)
    zfaces = gather_faces(z_x[:, :, 0], z_y[:, :, 0])
    zsub = (zfaces * live[..., None]).reshape(4, inner, loads).astype(jnp.bfloat16)
    image = jnp.einsum(
        "snk,skr->snr", schur.reshape(4, inner, inner), zsub, preferred_element_type=jnp.float32
    )
    return (z_x, z_y, image.astype(jnp.bfloat16).reshape(2, 2, 1, inner, loads))


def solution(mesh):
    return jax.shard_map(
        on_device,
        mesh=mesh,
        in_specs=(
            P("gx", "gy", "gz", None, None),
            P("gx", "gy", "gz", None, None),
            P("gx", "gy", "gz", None, None),
            P("gx", "gy", "gz", None),
            P("gx", "gy", "gz", None, None),
            P("gx", "gy", "gz", None, None),
            P("gx", "gy", "gz", None, None),
            P("gx", "gy", "gz", None),
            P("gx", "gy", "gz", None),
            P("gx", "gy", "gz", None),
            P(),
        ),
        out_specs=(
            P("gx", "gy", "gz", None, None),
            P("gx", "gy", "gz", None, None),
            P("gx", "gy", "gz", None, None),
        ),
        check_vma=False,
    )
```

profile of v0, /device:TPU:6, one launch (start us, length us, event | category | flops | bytes accessed | tf_op | source)
XLA Modules:
  0.0 522.4 jit_solution(4546723145671781828)
XLA Ops:
  7.2 2.4 fusion.25
  9.6 2.2 collective-permute-start.2
  15.8 7.1 %collective-permute-done.2 = f32[2,1,1,120,512]{4,3,1,0,2:T(8,128)} collective-permute-done((f32[2,1,1,120,512]{4,3,1,0,2:T(8,128)}, f32[2,1,1,120,512]{4,3,1,0,2:T(8,128)}, u32[]{:S(2)}, u32[]{:S(2)}) %collective-permute-start.2) | collective-permute-done | bytes 491552 | tf_op jit(solution)/shard_map/ppermute | solution.py:16
  22.9 1.2 collective-permute-done.3
  24.1 1.5 fusion.3
  25.9 1.1 copy-done.6
  27.0 1.5 maximum_add_fusion
  31.2 1.7 fusion.8
  33.0 153.5 %all-reduce.4.cloned.1.call-done = f32[512,512]{1,0:T(8,128)} async-done(((f32[512,512]{1,0:T(8,128)}), f32[512,512]{1,0:T(8,128)}) %all-reduce.4.cloned.1.call-update) | async-done | bytes 1048592 | tf_op jit(solution)/shard_map/psum | solution.py:75
  186.5 2.8 convolution_bitcast_fusion
  189.4 148.8 %all-reduce.6.cloned.1.call-done = f32[512,512]{0,1:T(8,128)} async-done(((f32[512,512]{0,1:T(8,128)}), f32[512,512]{0,1:T(8,128)}) %all-reduce.6.cloned.1.call-update) | async-done | bytes 1048592 | tf_op jit(solution)/shard_map/psum | solution.py:83
  339.2 64.1 %all-reduce.8.cloned.1.call-done = f32[512,512]{0,1:T(8,128)} async-done(((f32[512,512]{0,1:T(8,128)}), f32[512,512]{0,1:T(8,128)}) %all-reduce.8.cloned.1.call-update) | async-done | bytes 1048592 | tf_op jit(solution)/shard_map/psum | solution.py:84
  403.3 3.4 fusion.26
  406.7 1.6 fusion.5
  408.4 78.2 %all-gather.2.cloned.1.call-done = f32[512,512]{1,0:T(8,128)} async-done(((f32[16,512]{1,0:T(8,128)}), f32[512,512]{1,0:T(8,128)}) %all-gather.2.cloned.1.call-update) | async-done | bytes 1048592 | tf_op jit(solution)/shard_map/all_gather | solution.py:87
  486.6 2.0 convolution_convert_fusion
  489.3 1.4 copy-done.3
  490.7 1.3 convolution_add_fusion
  494.4 1.5 collective-permute-start.7
  496.2 1.3 copy.68
  497.6 9.4 %collective-permute-done.6 = f32[2,1,1,120,512]{4,3,0,2,1:T(8,128)S(1)} collective-permute-done((f32[2,1,1,120,512]{4,3,0,2,1:T(8,128)S(1)}, f32[2,1,1,120,512]{4,3,0,2,1:T(8,128)S(1)}, u32[]{:S(2)}, u32[]{:S(2)}) %collective-permute-start.6) | collective-permute-done | bytes 491552 | tf_op jit(solution)/shard_map/ppermute | solution.py:16
  507.0 1.5 collective-permute-done.7
  511.3 2.5 fusion.2
  513.8 1.5 fusion.4
  (80 shorter events, 14.8 us)
Async XLA Ops:
  7.2 482.1 %copy-start = (bf16[2,2,1,480,480]{4,3,2,1,0:T(8,128)(2,1)S(1)}, bf16[2,2,1,480,480]{4,3,2,1,0:T(8,128)(2,1)}, u32[]{:S(2)}) copy-start(bf16[2,2,1,480,480]{4,3,2,1,0:T(8,128)(2,1)} %param.15) | copy-start | bytes 5529604
  7.2 4.6 copy-start.5
  7.2 179.3 %all-reduce.4.cloned.1.call-start = ((), (), s32[]{:S(2)}) async-start(), calls=%async_computation | async-start | bytes 2097152 | tf_op jit(solution)/shard_map/psum | solution.py:75
  9.6 13.3 %collective-permute-start.2 = (f32[2,1,1,120,512]{4,3,1,0,2:T(8,128)}, f32[2,1,1,120,512]{4,3,1,0,2:T(8,128)}, u32[]{:S(2)}, u32[]{:S(2)}) collective-permute-start(f32[2,1,1,120,512]{4,3,1,0,2:T(8,128)} %get-tuple-element.35), channel_id=1, source_target_pairs={{0,32},{32,64},{64,96},{96,0},{1,33},{33,65},{65,97},{97,1},{2,34}... | collective-permute-start | bytes 1474568 | tf_op jit(solution)/shard_map/ppermute | solution.py:16
  11.8 12.3 %collective-permute-start.3 = (f32[2,1,1,120,512]{4,3,1,0,2:T(8,128)}, f32[2,1,1,120,512]{4,3,1,0,2:T(8,128)}, u32[]{:S(2)}, u32[]{:S(2)}) collective-permute-start(f32[2,1,1,120,512]{4,3,1,0,2:T(8,128)} %get-tuple-element.36), channel_id=1, source_target_pairs={{32,0},{64,32},{96,64},{0,96},{33,1},{65,33},{97,65},{1,97},{34,2}... | collective-permute-start | bytes 1474568 | tf_op jit(solution)/shard_map/ppermute | solution.py:17
  11.9 2.2 copy-start.13
  11.9 2.7 copy-start.14
  11.9 3.7 copy-start.12
  11.9 12.2 %copy-start.4 = (f32[2,3,1,120,512]{4,3,2,1,0:T(8,128)S(1)}, f32[2,3,1,120,512]{4,3,2,1,0:T(8,128)}, u32[]{:S(2)}) copy-start(f32[2,3,1,120,512]{4,3,2,1,0:T(8,128)} %param.12) | copy-start | bytes 4423684
  12.7 13.1 %collective-permute-start.1 = (f32[1,2,1,120,512]{4,3,0,1,2:T(8,128)}, f32[1,2,1,120,512]{4,3,0,1,2:T(8,128)}, u32[]{:S(2)}, u32[]{:S(2)}) collective-permute-start(f32[1,2,1,120,512]{4,3,0,1,2:T(8,128)} %copy.74), channel_id=1, source_target_pairs={{128,0},{0,128},{129,1},{1,129},{130,2},{2,130},{131,3},{3,131},{1... | collective-permute-start | bytes 1474568 | tf_op jit(solution)/shard_map/ppermute | solution.py:17
  13.5 12.3 %collective-permute-start = (f32[1,2,1,120,512]{4,3,0,1,2:T(8,128)}, f32[1,2,1,120,512]{4,3,0,1,2:T(8,128)}, u32[]{:S(2)}, u32[]{:S(2)}) collective-permute-start(f32[1,2,1,120,512]{4,3,0,1,2:T(8,128)} %copy.75), channel_id=1, source_target_pairs={{0,128},{128,0},{1,129},{129,1},{2,130},{130,2},{3,131},{131,3},{4... | collective-permute-start | bytes 1474568 | tf_op jit(solution)/shard_map/ppermute | solution.py:16
  29.3 1.9 copy-start.2
  31.2 155.3 %copy-start.10 = (f32[1,1,16,512]{3,2,1,0:T(8,128)S(1)}, f32[1,1,16,512]{3,2,1,0:T(8,128)}, u32[]{:S(2)}) copy-start(f32[1,1,16,512]{3,2,1,0:T(8,128)} %param.20) | copy-start | bytes 98308
  32.9 305.4 %all-reduce.6.cloned.1.call-start = ((), (), s32[]{:S(2)}) async-start(), calls=%async_computation.1 | async-start | bytes 2097152 | tf_op jit(solution)/shard_map/psum | solution.py:83
  33.0 305.6 %copy-start.11 = (f32[1,1,16,512]{3,2,1,0:T(8,128)S(1)}, f32[1,1,16,512]{3,2,1,0:T(8,128)}, u32[]{:S(2)}) copy-start(f32[1,1,16,512]{3,2,1,0:T(8,128)} %param.19) | copy-start | bytes 98308
  186.5 152.0 %copy-start.8 = (f32[512,512]{1,0:T(8,128)S(1)}, f32[512,512]{1,0:T(8,128)}, u32[]{:S(2)}) copy-start(f32[512,512]{1,0:T(8,128)} %all-reduce.4.cloned.1.call-done) | copy-start | bytes 3145732
  189.4 213.9 %all-reduce.8.cloned.1.call-start = ((), (), s32[]{:S(2)}) async-start(), calls=%async_computation.2 | async-start | bytes 2097152 | tf_op jit(solution)/shard_map/psum | solution.py:84
  338.3 148.3 %all-gather.2.cloned.1.call-start = ((), (), s32[]{:S(2)}) async-start(), calls=%async_computation.3 | async-start | bytes 1081344 | tf_op jit(solution)/shard_map/all_gather | solution.py:87
  488.5 2.1 copy-start.3
  492.5 3.3 collective-permute-start.5
  492.6 3.2 collective-permute-start.4
  493.7 13.3 %collective-permute-start.6 = (f32[2,1,1,120,512]{4,3,0,2,1:T(8,128)S(1)}, f32[2,1,1,120,512]{4,3,0,2,1:T(8,128)S(1)}, u32[]{:S(2)}, u32[]{:S(2)}) collective-permute-start(f32[2,1,1,120,512]{4,3,0,2,1:T(8,128)S(1)} %get-tuple-element.27), channel_id=1, source_target_pairs={{0,32},{32,64},{64,96},{96,0},{1,33},{33,65},{65,97},{97,1},{2,34}... | collective-permute-start | bytes 1474568 | tf_op jit(solution)/shard_map/ppermute | solution.py:16
  494.4 14.2 %collective-permute-start.7 = (f32[2,1,1,120,512]{4,3,0,2,1:T(8,128)S(1)}, f32[2,1,1,120,512]{4,3,0,2,1:T(8,128)S(1)}, u32[]{:S(2)}, u32[]{:S(2)}) collective-permute-start(f32[2,1,1,120,512]{4,3,0,2,1:T(8,128)S(1)} %get-tuple-element.28), channel_id=1, source_target_pairs={{32,0},{64,32},{96,64},{0,96},{33,1},{65,33},{97,65},{1,97},{34,2}... | collective-permute-start | bytes 1474568 | tf_op jit(solution)/shard_map/ppermute | solution.py:17
  513.8 2.1 copy-start.1
  (3 other events, 3.9 us)
Sparse Core Ops, SparseCore 0:
  33.0 153.4 all-reduce.3
  190.5 147.6 all-reduce.5
  340.6 62.6 all-reduce.7
  408.4 78.0 all-gather.1
where the time goes:
time: 523 us; the launch traced here: 522 us
  waiting for transfers between devices  464 us (89%)
  matrix products  17.2 us (3%)
  between operations  14.1 us (3%)
  local copies, waits for them, and re-layouts  13.3 us (3%)
  other arithmetic  8.02 us (2%)
  starting transfers between devices  5.73 us (1%)
    psum x1, waiting for transfers between devices, on_device(): column_res = lax.psum(column_part, 'gz')  154 us
    psum x1, waiting for transfers between devices, on_device(): column_top = lax.psum(top_part, 'gz')  149 us
    all_gather x1, waiting for transfers between devices, on_device(): column_vals = lax.all_gather(value_rows, 'gz', axis=0, tiled=True)  78.2 us
    psum x1, waiting for transfers between devices, on_device(): top_res = lax.psum(column_top, ('gx', 'gy'))  64.1 us
    ppermute x4, waiting for transfers between devices, with_halo(): before = lax.ppermute(last, axis, up)  16.6 us
  transfers between devices with their start and end apart: 12, of which 8 were waited for; matrix products, arithmetic and copies ran while one was open for 2% of the time, Pallas kernels for 0%

commit v1 on v0

v1 whole, which is shorter than its diff:
```python
import functools

import jax
import jax.numpy as jnp
from jax import lax
from jax.experimental import pallas as pl
from jax.experimental.pallas import tpu as pltpu
from jax.sharding import Mesh, PartitionSpec as P

BLK = 30
YS = 4
LANES = 128
WIDE = 256
F32 = jnp.float32
BF16 = jnp.bfloat16
HIGH = lax.Precision.HIGHEST
NT = (((1,), (1,)), ((), ()))
TN = (((0,), (0,)), ((), ()))


def call(body, outs, *args, grid=None, ins=None, specs=None, scratch=(), mib=16):
    extra = {} if grid is None else {"grid": grid, "in_specs": ins, "out_specs": specs}
    return pl.pallas_call(
        body,
        out_shape=outs,
        scratch_shapes=scratch,
        compiler_params=pltpu.CompilerParams(vmem_limit_bytes=mib << 20),
        **extra,
    )(*args)


def shape(*dims, dtype=F32):
    return jax.ShapeDtypeStruct(dims, dtype)


def dot(a, b, dims=(((1,), (0,)), ((), ())), precision=None):
    return lax.dot_general(a, b, dims, precision=precision, preferred_element_type=F32)


def parts_of(value):
    first = value.astype(BF16)
    rest = value - first.astype(F32)
    second = rest.astype(BF16)
    third = (rest - second.astype(F32)).astype(BF16)
    return first, second, third


def live_columns(counts, dofs):
    index = lax.broadcasted_iota(jnp.int32, (dofs, 1), 0)
    out = []
    for s in range(4):
        for f in range(4):
            out.append((index < counts[s, f] * BLK).astype(F32))
    return out


def scale_columns(counts, weights, dofs):
    turned = weights[...].reshape(16, dofs).T
    live = live_columns(counts, dofs)
    return [turned[:, i : i + 1] * live[i] for i in range(16)], live


def face_list(x, y, i, j):
    return (x[i][j], x[i + 1][j], y[j][i], y[j + 1][i])


def front_body(counts, cmap, weights, basis, rx, ry, xb, xa, yb, ya, msg, u):
    dofs = rx.shape[3]
    scale, _ = scale_columns(counts, weights, dofs)
    x = [
        [rx[0, j, 0] + xb[j] for j in range(2)],
        [rx[1, j, 0] for j in range(2)],
        [rx[2, j, 0] + xa[j] for j in range(2)],
    ]
    y = [
        [ry[i, 0, 0] + yb[i] for i in range(2)],
        [ry[i, 1, 0] for i in range(2)],
        [ry[i, 2, 0] + ya[i] for i in range(2)],
    ]
    local = basis.shape[2]
    for s in range(4):
        i, j = divmod(s, 2)
        faces = face_list(x, y, i, j)
        part = jnp.concatenate([faces[f] * scale[4 * s + f] for f in range(4)], 0).astype(BF16)
        u[s] = part
        g = dot(basis[s], part, TN)
        for c in range(msg.shape[0]):
            msg[c, s * local : (s + 1) * local] = g[:, c * LANES : (c + 1) * LANES]
    tile = cmap[...].astype(F32)
    for c in range(msg.shape[0]):
        msg[c, 4 * local :] = tile


def inverse_body(mat, u, out):
    for s in range(mat.shape[0]):
        out[s] = dot(mat[s], u[s])


def scatter_body(msg, out, maps):
    local = 4 * 64
    size = out.shape[2]
    total = None
    index = lax.broadcasted_iota(jnp.int32, (size, LANES), 0)
    for c in range(YS):
        tile = msg[c, local:]
        maps[c] = tile
        hot = jnp.concatenate(
            [(index == tile[h : h + 1].astype(jnp.int32)).astype(F32).astype(BF16) for h in range(2)], 1
        )
        three = jnp.concatenate(parts_of(msg[c, :local]), 1)
        made = dot(hot, three)
        total = made if total is None else total + made
    total = total[:, :LANES] + total[:, LANES : 2 * LANES] + total[:, 2 * LANES :]
    out[...] = total.T.reshape(out.shape)


def fill(full, mats, which):
    zs, rows = mats.shape[1], mats.shape[3]
    for c in range(YS):
        for z in range(zs):
            full[(z * YS + c) * rows : (z * YS + c + 1) * rows] = mats[c, z, which]


def down_body(parts, mats, g2, g3, full):
    total = parts[0]
    for z in range(1, parts.shape[0]):
        total = total + parts[z]
    g2[...] = total
    fill(full, mats, 1)
    made = dot(total, full[...], precision=HIGH)
    for k in range(g3.shape[0]):
        g3[k] = made


def up_body(parts, g2, top, mats, out, inv, bas):
    total = parts[0]
    for z in range(1, parts.shape[0]):
        total = total + parts[z]
    fill(inv, mats, 0)
    fill(bas, mats, 1)
    y3 = dot(total, top[...], NT, precision=HIGH)
    v2 = dot(g2[...], inv[...], NT, precision=HIGH) + dot(y3, bas[...], NT, precision=HIGH)
    for k in range(out.shape[0]):
        out[k] = v2


def select_body(values, maps, out):
    zs, part, size = values.shape
    v2 = values[...].reshape(zs * part, size).astype(BF16)
    index = lax.broadcasted_iota(jnp.int32, (LANES, size), 1)
    for c in range(YS):
        turned = maps[c].astype(jnp.int32).T
        for h in range(2):
            hot = (index == turned[:, h : h + 1]).astype(F32).astype(BF16)
            out[c, h * LANES : (h + 1) * LANES] = dot(hot, v2, NT)


def contrib_body(counts, weights, basis, w, v, x0, x1, x2, y0, y1, y2):
    dofs = x0.shape[1]
    scale, _ = scale_columns(counts, weights, dofs)
    local = basis.shape[2]
    parts = []
    for s in range(4):
        vs = jnp.concatenate([v[c, s * local : (s + 1) * local] for c in range(v.shape[0])], 1)
        full = w[s] + dot(basis[s], vs.astype(BF16))
        parts.append([full[f * dofs : (f + 1) * dofs] * scale[4 * s + f] for f in range(4)])
    for j in range(2):
        x0[j] = parts[j][0]
        x1[j] = parts[j][1] + parts[2 + j][0]
        x2[j] = parts[2 + j][1]
    for i in range(2):
        y0[i] = parts[2 * i][2]
        y1[i] = parts[2 * i][3] + parts[2 * i + 1][2]
        y2[i] = parts[2 * i + 1][3]


def image_body(counts, schur, x0, x1, x2, y0, y1, y2, xb, xa, yb, ya, zx, zy, image):
    dofs = x0.shape[1]
    live = live_columns(counts, dofs)
    x = [
        [x0[j] + xb[j] for j in range(2)],
        [x1[j] for j in range(2)],
        [x2[j] + xa[j] for j in range(2)],
    ]
    y = [
        [y0[i] + yb[i] for i in range(2)],
        [y1[i] for i in range(2)],
        [y2[i] + ya[i] for i in range(2)],
    ]
    for k in range(3):
        for j in range(2):
            zx[k, j, 0] = x[k][j]
            zy[j, k, 0] = y[k][j]
    for s in range(4):
        i, j = divmod(s, 2)
        faces = face_list(x, y, i, j)
        z = jnp.concatenate([faces[f] * live[4 * s + f] for f in range(4)], 0).astype(BF16)
        image[s] = dot(schur[s], z).astype(BF16)


def swap(value, axis, step):
    size = lax.axis_size(axis)
    return lax.ppermute(value, axis, [(i, (i + step) % size) for i in range(size)])


def to_all(blocks, axes):
    return lax.all_to_all(blocks, axes, 0, 0, tiled=False)


def spread(value, axes):
    size = lax.axis_size(axes)
    return to_all(jnp.broadcast_to(value[None], (size,) + value.shape), axes)


def on_device(
    resid_x,
    resid_y,
    face_weights,
    face_counts,
    neumann,
    schur,
    basis,
    coarse_map,
    column_inverse,
    column_basis,
    top_inverse,
):
    dofs, loads = resid_x.shape[3:]
    inner = neumann.shape[3]
    local = basis.shape[4]
    size = column_inverse.shape[3]
    zs = lax.axis_size("z")
    rows = column_inverse.shape[2]
    xb = swap(resid_x[2, :, 0], "gx", 1)
    xa = swap(resid_x[0, :, 0], "gx", -1)
    yb = swap(resid_y[:, 2, 0], "gy", 1)
    ya = swap(resid_y[:, 0, 0], "gy", -1)

    mats = jnp.concatenate([column_inverse[0, 0], column_basis[0, 0]], 0)
    mats = spread(mats, "z").reshape(zs * 2 * rows, size)
    mats = spread(mats, "y").reshape(YS, zs, 2, rows, size)

    counts = face_counts.reshape(4, 4)
    weights = face_weights.reshape(4, 4, dofs)
    nmat = neumann.reshape(4, inner, inner)
    smat = schur.reshape(4, inner, inner)
    bmat = basis.reshape(4, inner, local)
    cmap = jnp.pad(coarse_map.reshape(2, LANES), ((0, 6), (0, 0)))

    smem = pl.BlockSpec(memory_space=pltpu.SMEM)
    steps = loads // WIDE

    def whole(a):
        return pl.BlockSpec(a.shape, lambda n, d=a.ndim: (0,) * d)

    def lanes(*lead):
        return pl.BlockSpec(lead + (WIDE,), lambda n, d=len(lead): (0,) * d + (n,))

    nmsg = WIDE // LANES
    msg_rows = 4 * local + 8
    face = lanes(2, dofs)
    msg, u = call(
        front_body,
        (shape(YS, msg_rows, LANES), shape(4, inner, loads, dtype=BF16)),
        counts, cmap, weights, bmat, resid_x, resid_y, xb, xa, yb, ya,
        grid=(steps,),
        ins=[smem, whole(cmap), whole(weights), whole(bmat), lanes(3, 2, 1, dofs), lanes(2, 3, 1, dofs)]
        + [face] * 4,
        specs=(pl.BlockSpec((nmsg, msg_rows, LANES), lambda n: (n, 0, 0)), lanes(4, inner)),
        mib=24,
    )
    w = call(
        inverse_body,
        shape(4, inner, loads),
        nmat, u,
        grid=(4,),
        ins=[
            pl.BlockSpec((1, inner, inner), lambda n: (n, 0, 0)),
            pl.BlockSpec((1, inner, loads), lambda n: (n, 0, 0)),
        ],
        specs=pl.BlockSpec((1, inner, loads), lambda n: (n, 0, 0)),
        mib=12,
    )
    got = to_all(msg, "y")
    block = loads // YS // zs
    g2p, maps = call(scatter_body, (shape(zs, block, size), shape(YS, 8, LANES)), got)
    got = to_all(g2p, "z")
    cols = lax.axis_size("gx") * lax.axis_size("gy")
    g2, g3 = call(
        down_body, (shape(block, size), shape(cols, block, size)), got, mats,
        scratch=[pltpu.VMEM((size, size), F32)],
    )
    got = to_all(g3, ("gx", "gy"))
    v2 = call(
        up_body, shape(zs, block, size), got, g2, top_inverse, mats,
        scratch=[pltpu.VMEM((size, size), F32)] * 2,
    )
    got = to_all(v2, "z")
    sel = call(select_body, shape(YS, 4 * local, LANES), got, maps)
    v = to_all(sel, "y")
    fshape = shape(2, dofs, loads)
    x0, x1, x2, y0, y1, y2 = call(
        contrib_body,
        (fshape,) * 6,
        counts, weights, bmat, w, v,
        grid=(steps,),
        ins=[smem, whole(weights), whole(bmat), lanes(4, inner),
             pl.BlockSpec((nmsg, 4 * local, LANES), lambda n: (n, 0, 0))],
        specs=(face,) * 6,
        mib=24,
    )
    xb = swap(x2, "gx", 1)
    xa = swap(x0, "gx", -1)
    yb = swap(y2, "gy", 1)
    ya = swap(y0, "gy", -1)
    z_x, z_y, image = call(
        image_body,
        (shape(3, 2, 1, dofs, loads), shape(2, 3, 1, dofs, loads), shape(4, inner, loads, dtype=BF16)),
        counts, smat, x0, x1, x2, y0, y1, y2, xb, xa, yb, ya,
        grid=(steps,),
        ins=[smem, whole(smat)] + [face] * 10,
        specs=(lanes(3, 2, 1, dofs), lanes(2, 3, 1, dofs), lanes(4, inner)),
        mib=32,
    )
    return z_x, z_y, image.reshape(2, 2, 1, inner, loads)


def solution(mesh):
    sizes = mesh.devices.shape
    split = Mesh(
        mesh.devices.reshape(sizes[0], sizes[1], sizes[2] // YS, YS), ("gx", "gy", "z", "y")
    )
    gz = ("z", "y")
    five = P("gx", "gy", gz, None, None)
    four = P("gx", "gy", gz, None)
    return jax.shard_map(
        on_device,
        mesh=split,
        in_specs=(five, five, five, four, five, five, five, four, four, four, P()),
        out_specs=(five, five, five),
        check_vma=False,
    )
```

time: 523 us -> 168 us (0.32)
  waiting for transfers between devices: 464 us -> 46.8 us
  blocking collectives: 0 us -> 61.9 us
  starting transfers between devices: 5.73 us -> 24.7 us
  matrix products: 17.2 us -> 0 us
  Pallas kernels: 0 us -> 15.6 us
  between operations: 14.1 us -> 0.85 us
  other arithmetic: 8.02 us -> 0.64 us
    psum x3 -> x0, waiting for transfers between devices: 366 us -> none  [the longest x1 154 us: on_device(): column_res = lax.psum(column_part, 'gz')]
    all_gather x1 -> x0, waiting for transfers between devices: 78.2 us -> none  [on_device(): column_vals = lax.all_gather(value_rows, 'gz', axis=0, tiled=True)]
    all_to_all x0 -> x4, blocking collectives: none -> 61.9 us  [to_all(): return lax.all_to_all(blocks, axes, 0, 0, tiled=False)]
    all_to_all x0 -> x3, waiting for transfers between devices: none -> 26.4 us  [to_all(): return lax.all_to_all(blocks, axes, 0, 0, tiled=False)]
    dot_general x10 -> x0, matrix products: 17.2 us -> none  [the longest x1 3.39 us: on_device(): level_three = jnp.dot(top_inverse, top_res, precision=high)]
    all_to_all x0 -> x3, starting transfers between devices: none -> 16.4 us  [to_all(): return lax.all_to_all(blocks, axes, 0, 0, tiled=False)]
    pallas_call x0 -> x8, Pallas kernels: none -> 15.6 us  [call(): pl.pallas_call(body, out_shape=outs, scratch_shapes=scratch, compiler_par...]
  transfers between devices with their start and end apart: 12 -> 11, of which waited for: 8 -> 5; matrix products, arithmetic and copies ran while one was open for 2% -> 2% of each run, Pallas kernels for 0% -> 2%
where the time goes in v1:
time: 168 us; the launch traced here: 164 us
  blocking collectives  61.9 us (37%)
  waiting for transfers between devices  46.8 us (28%)
  starting transfers between devices  24.7 us (15%)
  Pallas kernels  15.6 us (9%)
  local copies, waits for them, and re-layouts  13.9 us (8%)
    all_to_all x4, blocking collectives, to_all(): return lax.all_to_all(blocks, axes, 0, 0, tiled=False)  61.9 us
    all_to_all x3, waiting for transfers between devices, to_all(): return lax.all_to_all(blocks, axes, 0, 0, tiled=False)  26.4 us
    ppermute x8, waiting for transfers between devices, swap(): lax.ppermute(value, axis, [(i, (i + step) % size) for i in range(size)])  20.4 us
    all_to_all x3, starting transfers between devices, to_all(): return lax.all_to_all(blocks, axes, 0, 0, tiled=False)  16.4 us
    pallas_call x8, Pallas kernels, call(): pl.pallas_call(body, out_shape=outs, scratch_shapes=scratch, compiler_par...  15.6 us
    unnamed x32, local copies, waits for them, and re-layouts  9.42 us
    ppermute x8, starting transfers between devices, swap(): lax.ppermute(value, axis, [(i, (i + step) % size) for i in range(size)])  8.34 us
  transfers between devices with their start and end apart: 11, of which 5 were waited for; matrix products, arithmetic and copies ran while one was open for 2% of the time, Pallas kernels for 2%

profile of v1, /device:TPU:6, one launch (start us, length us, event | category | flops | bytes accessed | tf_op | source)
XLA Modules:
  0.0 164.5 jit_solution(2100736035244683931)
XLA Ops:
  0.7 2.3 %slice_bitcast_fusion = (f32[2,120,512]{2,1,0:T(8,128)}, f32[2,120,512]{2,1,0:T(8,128)}) fusion(f32[3,2,1,120,512]{4,3,1,2,0:T(8,128)} %bitcast.29), kind=kLoop, calls=%fused_computation | loop fusion | bytes 1966080 | tf_op jit(solution)/shard_map/squeeze | solution.py:235
  5.4 2.4 %collective-permute-start.2 = (f32[2,120,512]{2,1,0:T(8,128)}, f32[2,120,512]{2,1,0:T(8,128)}, u32[]{:S(2)}, u32[]{:S(2)}) collective-permute-start(f32[2,120,512]{2,1,0:T(8,128)} %get-tuple-element.37), channel_id=1, source_target_pairs={{0,32},{32,64},{64,96},{96,0},{1,33},{33,65},{65,97},{97,1},{2,34}... | collective-permute-start | bytes 1474568 | tf_op jit(solution)/shard_map/ppermute | solution.py:203
  10.3 8.9 %collective-permute-done.3.ya = f32[2,120,512]{2,1,0:T(8,128)} collective-permute-done((f32[2,120,512]{2,1,0:T(8,128)}, f32[2,120,512]{2,1,0:T(8,128)}, u32[]{:S(2)}, u32[]{:S(2)}) %collective-permute-start.3) | collective-permute-done | bytes 491552 | tf_op jit(solution)/shard_map/ppermute | solution.py:203
  19.2 3.0 %shard_map.130 = (f32[4,264,128]{2,1,0:T(8,128)S(1)}, bf16[4,480,512]{2,1,0:T(8,128)(2,1)S(1)}) custom-call(s32[4,4]{1,0:T(4,128)S(1)} %bitcast.34, s32[8,128]{1,0:T(8,128)S(1)} %pad.4.cmap, f32[4,4,120]{2,1,0:T(4,128)S(1)} %bitcast.32, bf16[4,480,64]{2,1,0:T(8,128)(2,1)S(1)} %bitcast.27, f32[3,2,1,120,512]{4,3,2,1,0:T(8,128)S(1)} %copy-done.2, ...), custom_call_target="tpu_custom_call" | custom-call | tf_op jit(solution)/shard_map/pallas_call | solution.py:23
  24.3 4.5 %all-to-all-start = ((f32[4,264,128]{2,1,0:T(8,128)}), f32[4,264,128]{2,1,0:T(8,128)S(1)}, u32[]{:S(2)}, u32[]{:S(2)}) async-start(f32[4,264,128]{2,1,0:T(8,128)} %copy-done.9), calls=%async_computation | async-start | bytes 1081344 | tf_op jit(solution)/shard_map/all_to_all | solution.py:207
  28.8 8.9 %all-to-all-done.msg = f32[4,264,128]{2,1,0:T(8,128)S(1)} async-done(((f32[4,264,128]{2,1,0:T(8,128)}), f32[4,264,128]{2,1,0:T(8,128)S(1)}, u32[]{:S(2)}, u32[]{:S(2)}) %all-to-all-start) | async-done | bytes 540704 | tf_op jit(solution)/shard_map/all_to_all | solution.py:207
  38.6 8.5 %all-to-all-start.2 = ((f32[8,32,512]{2,1,0:T(8,128)}), f32[8,32,512]{2,1,0:T(8,128)S(1)}, u32[]{:S(2)}, u32[]{:S(2)}) async-start(f32[8,32,512]{2,1,0:T(8,128)} %broadcast_in_dim.6), calls=%async_computation.2 | async-start | bytes 1048576 | tf_op jit(solution)/shard_map/all_to_all | solution.py:207
  47.8 14.6 %all-to-all-done.2 = f32[8,32,512]{2,1,0:T(8,128)S(1)} async-done(((f32[8,32,512]{2,1,0:T(8,128)}), f32[8,32,512]{2,1,0:T(8,128)S(1)}, u32[]{:S(2)}, u32[]{:S(2)}) %all-to-all-start.2) | async-done | bytes 524320 | tf_op jit(solution)/shard_map/all_to_all | solution.py:207
  62.4 12.9 %all_to_all.35.parts = f32[8,16,512]{2,1,0:T(8,128)S(1)} all-to-all(f32[8,16,512]{2,1,0:T(8,128)S(1)} %get-tuple-element.20), channel_id=1, replica_groups=mesh['gx'=2,'gy'=4,'z'=8,'y'=4] {'z'}, dimensions={0} | all-to-all | bytes 524288 | tf_op jit(solution)/shard_map/all_to_all | solution.py:207
  75.5 24.7 %all_to_all.36 = f32[4,256,512]{2,1,0:T(8,128)S(1)} all-to-all(f32[4,256,512]{2,1,0:T(8,128)S(1)} %broadcast_in_dim.15), channel_id=1, replica_groups=mesh['gx'=2,'gy'=4,'z'=8,'y'=4] {'y'}, dimensions={0} | all-to-all | bytes 4194304 | tf_op jit(solution)/shard_map/all_to_all | solution.py:207
  100.9 9.9 %all_to_all.37.parts = f32[8,16,512]{2,1,0:T(8,128)S(1)} all-to-all(f32[8,16,512]{2,1,0:T(8,128)S(1)} %get-tuple-element.21), channel_id=1, replica_groups=mesh['gx'=2,'gy'=4,'z'=8,'y'=4] {'gx','gy'}, dimensions={0} | all-to-all | bytes 524288 | tf_op jit(solution)/shard_map/all_to_all | solution.py:207
  110.8 2.7 %shard_map.134 = f32[8,16,512]{2,1,0:T(8,128)S(1)} custom-call(f32[8,16,512]{2,1,0:T(8,128)S(1)} %all_to_all.37.parts, f32[16,512]{1,0:T(8,128)S(1)} %get-tuple-element.22.g2, f32[512,512]{1,0:T(8,128)S(1)} %copy-done.8, f32[4,8,2,16,512]{4,3,2,1,0:T(8,128)S(1)} %bitcast.26), custom_call_target="tpu_custom_call" | custom-call | tf_op jit(solution)/shard_map/pallas_call | solution.py:23
  113.5 14.3 %all_to_all.38.values = f32[8,16,512]{2,1,0:T(8,128)S(1)} all-to-all(f32[8,16,512]{2,1,0:T(8,128)S(1)} %shard_map.134), channel_id=1, replica_groups=mesh['gx'=2,'gy'=4,'z'=8,'y'=4] {'z'}, dimensions={0} | all-to-all | bytes 524288 | tf_op jit(solution)/shard_map/all_to_all | solution.py:207
  127.8 1.6 shard_map.135
  129.4 3.5 %all-to-all-start.6 = ((f32[4,256,128]{2,1,0:T(8,128)}), f32[4,256,128]{2,1,0:T(8,128)S(1)}, u32[]{:S(2)}, u32[]{:S(2)}) async-start(f32[4,256,128]{2,1,0:T(8,128)} %shard_map.135), calls=%async_computation.6 | async-start | bytes 1048576 | tf_op jit(solution)/shard_map/all_to_all | solution.py:207
  134.4 1.7 %shard_map.131.w = f32[4,480,512]{2,1,0:T(8,128)S(1)} custom-call(bf16[4,480,480]{2,1,0:T(8,128)(2,1)S(1)} %bitcast.31, bf16[4,480,512]{2,1,0:T(8,128)(2,1)S(1)} %copy-done.7), custom_call_target="tpu_custom_call" | custom-call | tf_op jit(solution)/shard_map/pallas_call | solution.py:23
  136.1 1.9 %copy-done = f32[4,480,512]{2,1,0:T(8,128)} copy-done((f32[4,480,512]{2,1,0:T(8,128)}, f32[4,480,512]{2,1,0:T(8,128)S(1)}, u32[]{:S(2)}) %copy-start) | copy-done | bytes 3932184
  138.0 2.9 %all-to-all-done.6.v = f32[4,256,128]{2,1,0:T(8,128)S(1)} async-done(((f32[4,256,128]{2,1,0:T(8,128)}), f32[4,256,128]{2,1,0:T(8,128)S(1)}, u32[]{:S(2)}, u32[]{:S(2)}) %all-to-all-start.6) | async-done | bytes 524320 | tf_op jit(solution)/shard_map/all_to_all | solution.py:207
  140.9 2.1 %copy-done.1 = f32[4,480,512]{2,1,0:T(8,128)S(1)} copy-done((f32[4,480,512]{2,1,0:T(8,128)S(1)}, f32[4,480,512]{2,1,0:T(8,128)}, u32[]{:S(2)}) %copy-start.1) | copy-done | bytes 3932184
  143.0 2.0 %shard_map.136 = (f32[2,120,512]{2,1,0:T(8,128)S(1)}, f32[2,120,512]{2,1,0:T(8,128)S(1)}, f32[2,120,512]{2,1,0:T(8,128)S(1)}, f32[2,120,512]{2,1,0:T(8,128)S(1)}...) custom-call(s32[4,4]{1,0:T(4,128)S(1)} %bitcast.35, f32[4,4,120]{2,1,0:T(4,128)S(1)} %bitcast.33, ...), custom_call_target="tpu_custom_call" | custom-call | tf_op jit(solution)/shard_map/pallas_call | solution.py:23
  145.6 2.2 %collective-permute-start.7 = (f32[2,120,512]{2,1,0:T(8,128)S(1)}, f32[2,120,512]{2,1,0:T(8,128)S(1)}, u32[]{:S(2)}, u32[]{:S(2)}) collective-permute-start(f32[2,120,512]{2,1,0:T(8,128)S(1)} %get-tuple-element.27.y0), channel_id=1, source_target_pairs={{0,96},{32,0},{64,32},{96,64},{1,97},{33,1},{65,33},{97,65},{2,98}... | collective-permute-start | bytes 1474568 | tf_op jit(solution)/shard_map/ppermute | solution.py:203
  147.8 1.9 %collective-permute-start.6 = (f32[2,120,512]{2,1,0:T(8,128)S(1)}, f32[2,120,512]{2,1,0:T(8,128)S(1)}, u32[]{:S(2)}, u32[]{:S(2)}) collective-permute-start(f32[2,120,512]{2,1,0:T(8,128)S(1)} %get-tuple-element.29.y2), channel_id=1, source_target_pairs={{0,32},{32,64},{64,96},{96,0},{1,33},{33,65},{65,97},{97,1},{2,34}... | collective-permute-start | bytes 1474568 | tf_op jit(solution)/shard_map/ppermute | solution.py:203
  149.6 11.5 %collective-permute-done.7.ya = f32[2,120,512]{2,1,0:T(8,128)S(1)} collective-permute-done((f32[2,120,512]{2,1,0:T(8,128)S(1)}, f32[2,120,512]{2,1,0:T(8,128)S(1)}, u32[]{:S(2)}, u32[]{:S(2)}) %collective-permute-start.7) | collective-permute-done | bytes 491552 | tf_op jit(solution)/shard_map/ppermute | solution.py:203
  161.1 3.4 %shard_map.137 = (f32[3,2,1,120,512]{4,3,2,1,0:T(8,128)}, f32[2,3,1,120,512]{4,3,2,1,0:T(8,128)}, bf16[4,480,512]{2,1,0:T(8,128)(2,1)}) custom-call(s32[4,4]{1,0:T(4,128)S(1)} %bitcast.36, bf16[4,480,480]{2,1,0:T(8,128)(2,1)S(1)} %bitcast.30, f32[2,120,512]{2,1,0:T(8,128)S(1)} %get-tuple-element.24.x0, f32[2,120,512]{2,1,0:T(8,128)S(1)} %get-tuple-element.25.x1, ...), custom_call_target="tpu_custom_call" | custom-call | tf_op jit(solution)/shard_map/pallas_call | solution.py:23
  (50 shorter events, 11.6 us)
Async XLA Ops:
  0.6 2.9 %copy-start.3 = (f32[2,3,1,120,512]{4,3,2,1,0:T(8,128)S(1)}, f32[2,3,1,120,512]{4,3,2,1,0:T(8,128)}, u32[]{:S(2)}) copy-start(f32[2,3,1,120,512]{4,3,2,1,0:T(8,128)} %ry.1) | copy-start | bytes 4423684
  0.6 7.7 %copy-start.14 = (s32[2,2,1,64]{3,2,1,0:T(1,128)S(1)}, s32[2,2,1,64]{3,2,1,0:T(1,128)}, u32[]{:S(2)}) copy-start(s32[2,2,1,64]{3,2,1,0:T(1,128)} %param.18) | copy-start | bytes 3076
  0.7 18.5 %copy-start.2 = (f32[3,2,1,120,512]{4,3,2,1,0:T(8,128)S(1)}, f32[3,2,1,120,512]{4,3,2,1,0:T(8,128)}, u32[]{:S(2)}) copy-start(f32[3,2,1,120,512]{4,3,2,1,0:T(8,128)} %rx.1) | copy-start | bytes 4423684
  0.7 18.5 %copy-start.10 = (f32[2,2,1,4,120]{4,3,2,1,0:T(4,128)S(1)}, f32[2,2,1,4,120]{4,3,2,1,0:T(4,128)}, u32[]{:S(2)}) copy-start(f32[2,2,1,4,120]{4,3,2,1,0:T(4,128)} %param.13) | copy-start | bytes 23044
  0.7 18.5 %copy-start.11 = (s32[2,2,1,4]{3,2,1,0:T(1,128)S(1)}, s32[2,2,1,4]{3,2,1,0:T(1,128)}, u32[]{:S(2)}) copy-start(s32[2,2,1,4]{3,2,1,0:T(1,128)} %param.14) | copy-start | bytes 196
  3.0 7.3 %collective-permute-start.1 = (f32[2,120,512]{2,1,0:T(8,128)}, f32[2,120,512]{2,1,0:T(8,128)}, u32[]{:S(2)}, u32[]{:S(2)}) collective-permute-start(f32[2,120,512]{2,1,0:T(8,128)} %get-tuple-element.38), channel_id=1, source_target_pairs={{0,128},{128,0},{1,129},{129,1},{2,130},{130,2},{3,131},{131,3},{4... | collective-permute-start | bytes 1474568 | tf_op jit(solution)/shard_map/ppermute | solution.py:203
  3.0 7.3 %collective-permute-start = (f32[2,120,512]{2,1,0:T(8,128)}, f32[2,120,512]{2,1,0:T(8,128)}, u32[]{:S(2)}, u32[]{:S(2)}) collective-permute-start(f32[2,120,512]{2,1,0:T(8,128)} %get-tuple-element.39), channel_id=1, source_target_pairs={{0,128},{128,0},{1,129},{129,1},{2,130},{130,2},{3,131},{131,3},{4... | collective-permute-start | bytes 1474568 | tf_op jit(solution)/shard_map/ppermute | solution.py:203
  4.5 14.7 %collective-permute-start.3 = (f32[2,120,512]{2,1,0:T(8,128)}, f32[2,120,512]{2,1,0:T(8,128)}, u32[]{:S(2)}, u32[]{:S(2)}) collective-permute-start(f32[2,120,512]{2,1,0:T(8,128)} %get-tuple-element.36), channel_id=1, source_target_pairs={{0,96},{32,0},{64,32},{96,64},{1,97},{33,1},{65,33},{97,65},{2,98}... | collective-permute-start | bytes 1474568 | tf_op jit(solution)/shard_map/ppermute | solution.py:203
  5.4 13.8 %collective-permute-start.2 = (f32[2,120,512]{2,1,0:T(8,128)}, f32[2,120,512]{2,1,0:T(8,128)}, u32[]{:S(2)}, u32[]{:S(2)}) collective-permute-start(f32[2,120,512]{2,1,0:T(8,128)} %get-tuple-element.37), channel_id=1, source_target_pairs={{0,32},{32,64},{64,96},{96,0},{1,33},{33,65},{65,97},{97,1},{2,34}... | collective-permute-start | bytes 1474568 | tf_op jit(solution)/shard_map/ppermute | solution.py:203
  19.2 9.5 %copy-start.12 = (f32[1,1,16,512]{3,2,1,0:T(8,128)S(1)}, f32[1,1,16,512]{3,2,1,0:T(8,128)}, u32[]{:S(2)}) copy-start(f32[1,1,16,512]{3,2,1,0:T(8,128)} %param.20) | copy-start | bytes 98308
  19.2 9.5 %copy-start.13 = (f32[1,1,16,512]{3,2,1,0:T(8,128)S(1)}, f32[1,1,16,512]{3,2,1,0:T(8,128)}, u32[]{:S(2)}) copy-start(f32[1,1,16,512]{3,2,1,0:T(8,128)} %param.19) | copy-start | bytes 98308
  24.3 13.4 %all-to-all-start = ((f32[4,264,128]{2,1,0:T(8,128)}), f32[4,264,128]{2,1,0:T(8,128)S(1)}, u32[]{:S(2)}, u32[]{:S(2)}) async-start(f32[4,264,128]{2,1,0:T(8,128)} %copy-done.9), calls=%async_computation | async-start | bytes 1081344 | tf_op jit(solution)/shard_map/all_to_all | solution.py:207
  38.6 23.8 %all-to-all-start.2 = ((f32[8,32,512]{2,1,0:T(8,128)}), f32[8,32,512]{2,1,0:T(8,128)S(1)}, u32[]{:S(2)}, u32[]{:S(2)}) async-start(f32[8,32,512]{2,1,0:T(8,128)} %broadcast_in_dim.6), calls=%async_computation.2 | async-start | bytes 1048576 | tf_op jit(solution)/shard_map/all_to_all | solution.py:207
  100.2 10.6 %copy-start.8 = (f32[512,512]{1,0:T(8,128)S(1)}, f32[512,512]{1,0:T(8,128)}, u32[]{:S(2)}) copy-start(f32[512,512]{1,0:T(8,128)} %top.1) | copy-start | bytes 3145732
  113.5 19.4 %copy-start.5 = (bf16[2,2,1,480,480]{4,3,2,1,0:T(8,128)(2,1)S(1)}, bf16[2,2,1,480,480]{4,3,2,1,0:T(8,128)(2,1)}, u32[]{:S(2)}) copy-start(bf16[2,2,1,480,480]{4,3,2,1,0:T(8,128)(2,1)} %param.15) | copy-start | bytes 5529604
  129.4 11.5 %all-to-all-start.6 = ((f32[4,256,128]{2,1,0:T(8,128)}), f32[4,256,128]{2,1,0:T(8,128)S(1)}, u32[]{:S(2)}, u32[]{:S(2)}) async-start(f32[4,256,128]{2,1,0:T(8,128)} %shard_map.135), calls=%async_computation.6 | async-start | bytes 1048576 | tf_op jit(solution)/shard_map/all_to_all | solution.py:207
  132.9 1.5 copy-start.7
  136.1 1.9 %copy-start = (f32[4,480,512]{2,1,0:T(8,128)}, f32[4,480,512]{2,1,0:T(8,128)S(1)}, u32[]{:S(2)}) copy-start(f32[4,480,512]{2,1,0:T(8,128)S(1)} %shard_map.131.w) | copy-start | bytes 11796484
  140.9 2.1 %copy-start.1 = (f32[4,480,512]{2,1,0:T(8,128)S(1)}, f32[4,480,512]{2,1,0:T(8,128)}, u32[]{:S(2)}) copy-start(f32[4,480,512]{2,1,0:T(8,128)} %copy-done) | copy-start | bytes 11796484
  143.0 18.1 %copy-start.4 = (bf16[2,2,1,480,480]{4,3,2,1,0:T(8,128)(2,1)S(1)}, bf16[2,2,1,480,480]{4,3,2,1,0:T(8,128)(2,1)}, u32[]{:S(2)}) copy-start(bf16[2,2,1,480,480]{4,3,2,1,0:T(8,128)(2,1)} %param.16) | copy-start | bytes 5529604
  145.0 4.6 %collective-permute-start.5 = (f32[2,120,512]{2,1,0:T(8,128)S(1)}, f32[2,120,512]{2,1,0:T(8,128)S(1)}, u32[]{:S(2)}, u32[]{:S(2)}) collective-permute-start(f32[2,120,512]{2,1,0:T(8,128)S(1)} %get-tuple-element.24.x0), channel_id=1, source_target_pairs={{0,128},{128,0},{1,129},{129,1},{2,130},{130,2},{3,131},{131,3},{4... | collective-permute-start | bytes 1474568 | tf_op jit(solution)/shard_map/ppermute | solution.py:203
  145.1 4.5 %collective-permute-start.4 = (f32[2,120,512]{2,1,0:T(8,128)S(1)}, f32[2,120,512]{2,1,0:T(8,128)S(1)}, u32[]{:S(2)}, u32[]{:S(2)}) collective-permute-start(f32[2,120,512]{2,1,0:T(8,128)S(1)} %get-tuple-element.26.x2), channel_id=1, source_target_pairs={{0,128},{128,0},{1,129},{129,1},{2,130},{130,2},{3,131},{131,3},{4... | collective-permute-start | bytes 1474568 | tf_op jit(solution)/shard_map/ppermute | solution.py:203
  145.6 15.5 %collective-permute-start.7 = (f32[2,120,512]{2,1,0:T(8,128)S(1)}, f32[2,120,512]{2,1,0:T(8,128)S(1)}, u32[]{:S(2)}, u32[]{:S(2)}) collective-permute-start(f32[2,120,512]{2,1,0:T(8,128)S(1)} %get-tuple-element.27.y0), channel_id=1, source_target_pairs={{0,96},{32,0},{64,32},{96,64},{1,97},{33,1},{65,33},{97,65},{2,98}... | collective-permute-start | bytes 1474568 | tf_op jit(solution)/shard_map/ppermute | solution.py:203
  147.8 13.3 %collective-permute-start.6 = (f32[2,120,512]{2,1,0:T(8,128)S(1)}, f32[2,120,512]{2,1,0:T(8,128)S(1)}, u32[]{:S(2)}, u32[]{:S(2)}) collective-permute-start(f32[2,120,512]{2,1,0:T(8,128)S(1)} %get-tuple-element.29.y2), channel_id=1, source_target_pairs={{0,32},{32,64},{64,96},{96,0},{1,33},{33,65},{65,97},{97,1},{2,34}... | collective-permute-start | bytes 1474568 | tf_op jit(solution)/shard_map/ppermute | solution.py:203
  (2 other events, 2.1 us)

commit v2 on v1

--- a/solution.py
+++ b/solution.py
@@ -1,11 +1,10 @@
-import functools
-
 import jax
 import jax.numpy as jnp
 from jax import lax
 from jax.experimental import pallas as pl
 from jax.experimental.pallas import tpu as pltpu
 from jax.sharding import Mesh, PartitionSpec as P
+
 
 BLK = 30
 YS = 4
@@ -19,7 +18,11 @@
 
 
 def call(body, outs, *args, grid=None, ins=None, specs=None, scratch=(), mib=16):
-    extra = {} if grid is None else {"grid": grid, "in_specs": ins, "out_specs": specs}
+    extra = {}
+    if ins is not None:
+        extra["in_specs"] = ins
+    if grid is not None:
+        extra.update(grid=grid, out_specs=specs)
     return pl.pallas_call(
         body,
         out_shape=outs,
@@ -85,15 +88,34 @@
         u[s] = part
         g = dot(basis[s], part, TN)
         for c in range(msg.shape[0]):
-            msg[c, s * local : (s + 1) * local] = g[:, c * LANES : (c + 1) * LANES]
+            msg[c, (2 * j + i) * local : (2 * j + i + 1) * local] = g[:, c * LANES : (c + 1) * LANES]
     tile = cmap[...].astype(F32)
     for c in range(msg.shape[0]):
         msg[c, 4 * local :] = tile
 
 
-def inverse_body(mat, u, out):
-    for s in range(mat.shape[0]):
-        out[s] = dot(mat[s], u[s])
+def inverse_body(counts, weights, basis, mat, u, out, low, high):
+    dofs, loads = low.shape[1], u.shape[2]
+    local = basis.shape[2]
+    s = pl.program_id(0)
+    made = dot(mat[0], u[0])
+    out[0] = made
+    turned = weights[0].T
+    index = lax.broadcasted_iota(jnp.int32, (dofs, 1), 0)
+
+    def edge(ref, f):
+        scale = turned[:, f : f + 1] * (index < counts[s, f] * BLK).astype(F32)
+        ref[0, :, :loads] = made[f * dofs : (f + 1) * dofs] * scale
+        ref[0, :, loads : loads + local] = basis[0, f * dofs : (f + 1) * dofs].astype(F32)
+        ref[0, :, loads + local :] = jnp.broadcast_to(scale, (dofs, LANES - local))
+
+    @pl.when(s % 2 == 0)
+    def _():
+        edge(low, 2)
+
+    @pl.when(s % 2 == 1)
+    def _():
+        edge(high, 3)
 
 
 def scatter_body(msg, out, maps):
@@ -114,32 +136,38 @@
     out[...] = total.T.reshape(out.shape)
 
 
-def fill(full, mats, which):
-    zs, rows = mats.shape[1], mats.shape[3]
-    for c in range(YS):
+def fill(full, place, mats, which):
+    zs, rows = mats[0].shape[0], mats[0].shape[2]
+    for k in range(YS):
+        c = lax.rem(place[0] + YS - k, YS)
         for z in range(zs):
-            full[(z * YS + c) * rows : (z * YS + c + 1) * rows] = mats[c, z, which]
-
-
-def down_body(parts, mats, g2, g3, full):
+            start = pl.multiple_of((z * YS + c) * rows, rows)
+            full[pl.ds(start, rows)] = mats[k][z, which]
+
+
+def down_body(place, parts, m0, m1, m2, m3, g2, g3, full):
     total = parts[0]
     for z in range(1, parts.shape[0]):
         total = total + parts[z]
     g2[...] = total
-    fill(full, mats, 1)
+    fill(full, place, (m0, m1, m2, m3), 1)
     made = dot(total, full[...], precision=HIGH)
     for k in range(g3.shape[0]):
         g3[k] = made
 
 
-def up_body(parts, g2, top, mats, out, inv, bas):
+def level_body(place, g2, m0, m1, m2, m3, y2, full):
+    fill(full, place, (m0, m1, m2, m3), 0)
+    y2[...] = dot(g2[...], full[...], NT, precision=HIGH)
+
+
+def up_body(place, parts, y2, top, m0, m1, m2, m3, out, full):
     total = parts[0]
     for z in range(1, parts.shape[0]):
         total = total + parts[z]
-    fill(inv, mats, 0)
-    fill(bas, mats, 1)
+    fill(full, place, (m0, m1, m2, m3), 1)
     y3 = dot(total, top[...], NT, precision=HIGH)
-    v2 = dot(g2[...], inv[...], NT, precision=HIGH) + dot(y3, bas[...], NT, precision=HIGH)
+    v2 = y2[...] + dot(y3, full[...], NT, precision=HIGH)
     for k in range(out.shape[0]):
         out[k] = v2
 
@@ -161,7 +189,9 @@
     local = basis.shape[2]
     parts = []
     for s in range(4):
-        vs = jnp.concatenate([v[c, s * local : (s + 1) * local] for c in range(v.shape[0])], 1)
+        i, j = divmod(s, 2)
+        q = (2 * j + i) * local
+        vs = jnp.concatenate([v[c, q : q + local] for c in range(v.shape[0])], 1)
         full = w[s] + dot(basis[s], vs.astype(BF16))
         parts.append([full[f * dofs : (f + 1) * dofs] * scale[4 * s + f] for f in range(4)])
     for j in range(2):
@@ -174,9 +204,20 @@
         y2[i] = parts[2 * i + 1][3]
 
 
-def image_body(counts, schur, x0, x1, x2, y0, y1, y2, xb, xa, yb, ya, zx, zy, image):
+def beyond(edge, extra, v, i):
+    local = v.shape[1] // 2
+    vs = jnp.concatenate([v[c, i * local : (i + 1) * local] for c in range(v.shape[0])], 1)
+    other = extra[i]
+    return edge[i] + dot(other[:, :local].astype(BF16), vs.astype(BF16)) * other[:, local : local + 1]
+
+
+def image_body(
+    counts, schur, x0, x1, x2, y0, y1, y2, xb, xa, eb, ea, fb, fa, vb, va, zx, zy, image
+):
     dofs = x0.shape[1]
     live = live_columns(counts, dofs)
+    yb = [beyond(eb, fb, vb, i) for i in range(2)]
+    ya = [beyond(ea, fa, va, i) for i in range(2)]
     x = [
         [x0[j] + xb[j] for j in range(2)],
         [x1[j] for j in range(2)],
@@ -231,23 +272,26 @@
     size = column_inverse.shape[3]
     zs = lax.axis_size("z")
     rows = column_inverse.shape[2]
+    yb = swap(resid_y[:, 2, 0], "gy", 1)
+    ya = swap(resid_y[:, 0, 0], "gy", -1)
     xb = swap(resid_x[2, :, 0], "gx", 1)
     xa = swap(resid_x[0, :, 0], "gx", -1)
-    yb = swap(resid_y[:, 2, 0], "gy", 1)
-    ya = swap(resid_y[:, 0, 0], "gy", -1)
 
     mats = jnp.concatenate([column_inverse[0, 0], column_basis[0, 0]], 0)
-    mats = spread(mats, "z").reshape(zs * 2 * rows, size)
-    mats = spread(mats, "y").reshape(YS, zs, 2, rows, size)
+    mats = spread(mats, "z").reshape(zs, 2, rows, size)
+    mats = [mats] + [swap(mats, "y", k) for k in range(1, YS)]
+    place = lax.axis_index("y").reshape(1)
 
     counts = face_counts.reshape(4, 4)
     weights = face_weights.reshape(4, 4, dofs)
     nmat = neumann.reshape(4, inner, inner)
     smat = schur.reshape(4, inner, inner)
     bmat = basis.reshape(4, inner, local)
-    cmap = jnp.pad(coarse_map.reshape(2, LANES), ((0, 6), (0, 0)))
+    cmap = coarse_map.reshape(2, 2, local).transpose(1, 0, 2).reshape(2, LANES)
+    cmap = jnp.pad(cmap, ((0, 6), (0, 0)))
 
     smem = pl.BlockSpec(memory_space=pltpu.SMEM)
+    vmem = pl.BlockSpec(memory_space=pltpu.VMEM)
     steps = loads // WIDE
 
     def whole(a):
@@ -255,6 +299,9 @@
 
     def lanes(*lead):
         return pl.BlockSpec(lead + (WIDE,), lambda n, d=len(lead): (0,) * d + (n,))
+
+    def each(*tail):
+        return pl.BlockSpec((1,) + tail, lambda n, d=len(tail): (n,) + (0,) * d)
 
     nmsg = WIDE // LANES
     msg_rows = 4 * local + 8
@@ -269,35 +316,41 @@
         specs=(pl.BlockSpec((nmsg, msg_rows, LANES), lambda n: (n, 0, 0)), lanes(4, inner)),
         mib=24,
     )
-    w = call(
+    pair = pl.BlockSpec((1, dofs, loads + LANES), lambda n: (n // 2, 0, 0))
+    w, low, high = call(
         inverse_body,
-        shape(4, inner, loads),
-        nmat, u,
+        (shape(4, inner, loads),) + (shape(2, dofs, loads + LANES),) * 2,
+        counts, weights, bmat, nmat, u,
         grid=(4,),
-        ins=[
-            pl.BlockSpec((1, inner, inner), lambda n: (n, 0, 0)),
-            pl.BlockSpec((1, inner, loads), lambda n: (n, 0, 0)),
-        ],
-        specs=pl.BlockSpec((1, inner, loads), lambda n: (n, 0, 0)),
-        mib=12,
-    )
+        ins=[smem, each(4, dofs), each(inner, local), each(inner, inner), each(inner, loads)],
+        specs=(each(inner, loads), pair, pair),
+        mib=16,
+    )
+    eb = swap(high, "gy", 1)
+    ea = swap(low, "gy", -1)
     got = to_all(msg, "y")
     block = loads // YS // zs
     g2p, maps = call(scatter_body, (shape(zs, block, size), shape(YS, 8, LANES)), got)
     got = to_all(g2p, "z")
     cols = lax.axis_size("gx") * lax.axis_size("gy")
+    full = [pltpu.VMEM((size, size), F32)]
     g2, g3 = call(
-        down_body, (shape(block, size), shape(cols, block, size)), got, mats,
-        scratch=[pltpu.VMEM((size, size), F32)],
+        down_body, (shape(block, size), shape(cols, block, size)), place, got, *mats,
+        ins=[smem] + [vmem] * 5, scratch=full,
     )
     got = to_all(g3, ("gx", "gy"))
+    y2 = call(
+        level_body, shape(block, size), place, g2, *mats, ins=[smem] + [vmem] * 5, scratch=full
+    )
     v2 = call(
-        up_body, shape(zs, block, size), got, g2, top_inverse, mats,
-        scratch=[pltpu.VMEM((size, size), F32)] * 2,
+        up_body, shape(zs, block, size), place, got, y2, top_inverse, *mats,
+        ins=[smem] + [vmem] * 7, scratch=full,
     )
     got = to_all(v2, "z")
     sel = call(select_body, shape(YS, 4 * local, LANES), got, maps)
     v = to_all(sel, "y")
+    vb = swap(v[:, 2 * local :], "gy", 1)
+    va = swap(v[:, : 2 * local], "gy", -1)
     fshape = shape(2, dofs, loads)
     x0, x1, x2, y0, y1, y2 = call(
         contrib_body,
@@ -311,14 +364,14 @@
     )
     xb = swap(x2, "gx", 1)
     xa = swap(x0, "gx", -1)
-    yb = swap(y2, "gy", 1)
-    ya = swap(y0, "gy", -1)
+    extra = pl.BlockSpec((2, dofs, LANES), lambda n: (0, 0, loads // LANES))
+    vspec = pl.BlockSpec((nmsg, 2 * local, LANES), lambda n: (n, 0, 0))
     z_x, z_y, image = call(
         image_body,
         (shape(3, 2, 1, dofs, loads), shape(2, 3, 1, dofs, loads), shape(4, inner, loads, dtype=BF16)),
-        counts, smat, x0, x1, x2, y0, y1, y2, xb, xa, yb, ya,
+        counts, smat, x0, x1, x2, y0, y1, y2, xb, xa, eb, ea, eb, ea, vb, va,
         grid=(steps,),
-        ins=[smem, whole(smat)] + [face] * 10,
+        ins=[smem, whole(smat)] + [face] * 10 + [extra] * 2 + [vspec] * 2,
         specs=(lanes(3, 2, 1, dofs), lanes(2, 3, 1, dofs), lanes(4, inner)),
         mib=32,
     )

time: 168 us -> 153 us (0.911)
  the two profiles are of different devices: /device:TPU:6 before, /device:TPU:8 now
where the time goes in v2:
time: 153 us; the launch traced here: 152 us
  waiting for transfers between devices  57 us (37%)
  starting transfers between devices  44 us (29%)
  Pallas kernels  19.7 us (13%)
  blocking collectives  15 us (10%)
  local copies, waits for them, and re-layouts  14.6 us (10%)
    all_to_all x5, starting transfers between devices, to_all(): return lax.all_to_all(blocks, axes, 0, 0, tiled=False)  32.1 us
    ppermute x13, waiting for transfers between devices, swap(): lax.ppermute(value, axis, [(i, (i + step) % size) for i in range(size)])  30.2 us
    all_to_all x5, waiting for transfers between devices, to_all(): return lax.all_to_all(blocks, axes, 0, 0, tiled=False)  26.8 us
    pallas_call x9, Pallas kernels, call(): pl.pallas_call(body, out_shape=outs, scratch_shapes=scratch, compiler_par...  19.7 us
    all_to_all x1, blocking collectives, to_all(): return lax.all_to_all(blocks, axes, 0, 0, tiled=False)  15 us
    ppermute x13, starting transfers between devices, swap(): lax.ppermute(value, axis, [(i, (i + step) % size) for i in range(size)])  11.9 us
    unnamed x29, local copies, waits for them, and re-layouts  11.6 us
  transfers between devices with their start and end apart: 18, of which 9 were waited for; matrix products, arithmetic and copies ran while one was open for 2% of the time, Pallas kernels for 7%

profile of v2, /device:TPU:8, one launch (start us, length us, event | category | flops | bytes accessed | tf_op | source)
XLA Modules:
  0.0 152.0 jit_solution(9715654645605698893)
XLA Ops:
  2.4 8.5 %all-to-all-start.2 = ((f32[8,32,512]{2,1,0:T(8,128)}), f32[8,32,512]{2,1,0:T(8,128)S(1)}, u32[]{:S(2)}, u32[]{:S(2)}) async-start(f32[8,32,512]{2,1,0:T(8,128)} %broadcast_in_dim.2), calls=%async_computation.2 | async-start | bytes 1048576 | tf_op jit(solution)/shard_map/all_to_all | solution.py:248
  13.6 2.8 %collective-permute-start.3 = (f32[2,120,512]{2,1,0:T(8,128)}, f32[2,120,512]{2,1,0:T(8,128)}, u32[]{:S(2)}, u32[]{:S(2)}) collective-permute-start(f32[2,120,512]{2,1,0:T(8,128)} %get-tuple-element.42), channel_id=1, source_target_pairs={{0,96},{32,0},{64,32},{96,64},{1,97},{33,1},{65,33},{97,65},{2,98}... | collective-permute-start | bytes 1474568 | tf_op jit(solution)/shard_map/ppermute | solution.py:244
  17.7 9.5 %collective-permute-done.3.ya = f32[2,120,512]{2,1,0:T(8,128)} collective-permute-done((f32[2,120,512]{2,1,0:T(8,128)}, f32[2,120,512]{2,1,0:T(8,128)}, u32[]{:S(2)}, u32[]{:S(2)}) %collective-permute-start.3) | collective-permute-done | bytes 491552 | tf_op jit(solution)/shard_map/ppermute | solution.py:244
  27.2 3.4 %collective-permute-done.2.yb = f32[2,120,512]{2,1,0:T(8,128)} collective-permute-done((f32[2,120,512]{2,1,0:T(8,128)}, f32[2,120,512]{2,1,0:T(8,128)}, u32[]{:S(2)}, u32[]{:S(2)}) %collective-permute-start.2) | collective-permute-done | bytes 491552 | tf_op jit(solution)/shard_map/ppermute | solution.py:244
  32.0 2.7 %shard_map.130 = (f32[4,264,128]{2,1,0:T(8,128)S(1)}, bf16[4,480,512]{2,1,0:T(8,128)(2,1)S(1)}) custom-call(s32[4,4]{1,0:T(4,128)S(1)} %bitcast.43, s32[8,128]{1,0:T(8,128)S(1)} %pad.4.cmap, f32[4,4,120]{2,1,0:T(4,128)S(1)} %bitcast.40, bf16[4,480,64]{2,1,0:T(8,128)(2,1)S(1)} %bitcast.34, f32[3,2,1,120,512]{4,3,2,1,0:T(8,128)S(1)} %copy-done, ...), custom_call_target="tpu_custom_call" | custom-call | tf_op jit(solution)/shard_map/pallas_call | solution.py:26
  36.8 4.9 %all-to-all-start = ((f32[4,264,128]{2,1,0:T(8,128)}), f32[4,264,128]{2,1,0:T(8,128)S(1)}, u32[]{:S(2)}, u32[]{:S(2)}) async-start(f32[4,264,128]{2,1,0:T(8,128)} %copy-done.10), calls=%async_computation | async-start | bytes 1081344 | tf_op jit(solution)/shard_map/all_to_all | solution.py:248
  41.8 2.9 %collective-permute-start.5 = (f32[8,2,16,512]{3,2,1,0:T(8,128)S(1)}, f32[8,2,16,512]{3,2,1,0:T(8,128)S(1)}, u32[]{:S(2)}, u32[]{:S(2)}) collective-permute-start(f32[8,2,16,512]{3,2,1,0:T(8,128)S(1)} %bitcast.29), channel_id=1, source_target_pairs={{0,2},{1,3},{2,0},{3,1},{4,6},{5,7},{6,4},{7,5},{8,10},{9,11},{10,... | collective-permute-start | bytes 1572872 | tf_op jit(solution)/shard_map/ppermute | solution.py:244
  46.5 10.6 %all-to-all-done.msg = f32[4,264,128]{2,1,0:T(8,128)S(1)} async-done(((f32[4,264,128]{2,1,0:T(8,128)}), f32[4,264,128]{2,1,0:T(8,128)S(1)}, u32[]{:S(2)}, u32[]{:S(2)}) %all-to-all-start) | async-done | bytes 540704 | tf_op jit(solution)/shard_map/all_to_all | solution.py:248
  58.5 7.2 %all-to-all-start.1 = ((f32[8,16,512]{2,1,0:T(8,128)}), f32[8,16,512]{2,1,0:T(8,128)S(1)}, u32[]{:S(2)}, u32[]{:S(2)}) async-start(f32[8,16,512]{2,1,0:T(8,128)} %get-tuple-element.24), calls=%async_computation.1 | async-start | bytes 524288 | tf_op jit(solution)/shard_map/all_to_all | solution.py:248
  65.7 10.5 %all-to-all-done.1.parts = f32[8,16,512]{2,1,0:T(8,128)S(1)} async-done(((f32[8,16,512]{2,1,0:T(8,128)}), f32[8,16,512]{2,1,0:T(8,128)S(1)}, u32[]{:S(2)}, u32[]{:S(2)}) %all-to-all-start.1) | async-done | bytes 262176 | tf_op jit(solution)/shard_map/all_to_all | solution.py:248
  77.6 3.4 %all-to-all-start.3 = ((f32[8,16,512]{2,1,0:T(8,128)}), f32[8,16,512]{2,1,0:T(8,128)S(1)}, u32[]{:S(2)}, u32[]{:S(2)}) async-start(f32[8,16,512]{2,1,0:T(8,128)} %get-tuple-element.25), calls=%async_computation.3 | async-start | bytes 524288 | tf_op jit(solution)/shard_map/all_to_all | solution.py:248
  82.1 5.7 %all-to-all-done.3.parts = f32[8,16,512]{2,1,0:T(8,128)S(1)} async-done(((f32[8,16,512]{2,1,0:T(8,128)}), f32[8,16,512]{2,1,0:T(8,128)S(1)}, u32[]{:S(2)}, u32[]{:S(2)}) %all-to-all-start.3) | async-done | bytes 262176 | tf_op jit(solution)/shard_map/all_to_all | solution.py:248
  89.1 1.9 %shard_map.135 = f32[8,16,512]{2,1,0:T(8,128)S(1)} custom-call(s32[1]{0:T(128)} %bitcast.12.place, f32[8,16,512]{2,1,0:T(8,128)S(1)} %all-to-all-done.3.parts, f32[16,512]{1,0:T(8,128)S(1)} %shard_map.134.y2, f32[512,512]{1,0:T(8,128)S(1)} %copy-done.9, f32[8,2,16,512]{3,2,1,0:T(8,128)S(1)} %bitcast.33, f32[8,2,16,512]{3,2,1,0:T(8,128)S(1)} %collective-permute-done.4.m1, ...), custom_call_target="tpu_custom_call" | custom-call | tf_op jit(solution)/shard_map/pallas_call | solution.py:26
  91.0 15.0 %all_to_all.30.values = f32[8,16,512]{2,1,0:T(8,128)S(1)} all-to-all(f32[8,16,512]{2,1,0:T(8,128)S(1)} %shard_map.135), channel_id=1, replica_groups=mesh['gx'=2,'gy'=4,'z'=8,'y'=4] {'z'}, dimensions={0} | all-to-all | bytes 524288 | tf_op jit(solution)/shard_map/all_to_all | solution.py:248
  107.6 8.1 %all-to-all-start.5 = ((f32[4,256,128]{2,1,0:T(8,128)}), f32[4,256,128]{2,1,0:T(8,128)S(1)}, u32[]{:S(2)}, u32[]{:S(2)}) async-start(f32[4,256,128]{2,1,0:T(8,128)} %shard_map.136), calls=%async_computation.5 | async-start | bytes 1048576 | tf_op jit(solution)/shard_map/all_to_all | solution.py:248
  117.3 3.8 %shard_map.131 = (f32[4,480,512]{2,1,0:T(8,128)S(1)}, f32[2,120,640]{2,1,0:T(8,128)}, f32[2,120,640]{2,1,0:T(8,128)}) custom-call(s32[4,4]{1,0:T(4,128)S(1)} %bitcast.44, f32[4,4,120]{2,1,0:T(4,128)S(1)} %bitcast.41, bf16[4,480,64]{2,1,0:T(8,128)(2,1)S(1)} %bitcast.35, bf16[4,480,480]{2,1,0:T(8,128)(2,1)S(1)} %bitcast.38, bf16[4,480,512]{2,1,0:T(8,128)(2,1)S(1)} %copy-done.8), custom_call_target="tpu_custom_call" | custom-call | tf_op jit(solution)/shard_map/pallas_call | solution.py:26
  121.1 1.9 %copy-done.3 = f32[4,480,512]{2,1,0:T(8,128)} copy-done((f32[4,480,512]{2,1,0:T(8,128)}, f32[4,480,512]{2,1,0:T(8,128)S(1)}, u32[]{:S(2)}) %copy-start.3) | copy-done | bytes 3932184
  123.9 2.4 %collective-permute-start.10 = (f32[2,120,640]{2,1,0:T(8,128)}, f32[2,120,640]{2,1,0:T(8,128)S(1)}, u32[]{:S(2)}, u32[]{:S(2)}) collective-permute-start(f32[2,120,640]{2,1,0:T(8,128)} %get-tuple-element.35), channel_id=1, source_target_pairs={{0,96},{32,0},{64,32},{96,64},{1,97},{33,1},{65,33},{97,65},{2,98}... | collective-permute-start | bytes 1843208 | tf_op jit(solution)/shard_map/ppermute | solution.py:244
  126.2 2.1 %copy-done.4 = f32[4,480,512]{2,1,0:T(8,128)S(1)} copy-done((f32[4,480,512]{2,1,0:T(8,128)S(1)}, f32[4,480,512]{2,1,0:T(8,128)}, u32[]{:S(2)}) %copy-start.4) | copy-done | bytes 3932184
  128.3 2.0 %shard_map.137 = (f32[2,120,512]{2,1,0:T(8,128)S(1)}, f32[2,120,512]{2,1,0:T(8,128)S(1)}, f32[2,120,512]{2,1,0:T(8,128)S(1)}, f32[2,120,512]{2,1,0:T(8,128)S(1)}...) custom-call(s32[4,4]{1,0:T(4,128)S(1)} %bitcast.45, f32[4,4,120]{2,1,0:T(4,128)S(1)} %bitcast.42, ...), custom_call_target="tpu_custom_call" | custom-call | tf_op jit(solution)/shard_map/pallas_call | solution.py:26
  131.1 8.9 %collective-permute-done.9.eb.fb = f32[2,120,640]{2,1,0:T(8,128)S(1)} collective-permute-done((f32[2,120,640]{2,1,0:T(8,128)}, f32[2,120,640]{2,1,0:T(8,128)S(1)}, u32[]{:S(2)}, u32[]{:S(2)}) %collective-permute-start.9) | collective-permute-done | bytes 614432 | tf_op jit(solution)/shard_map/ppermute | solution.py:244
  140.8 4.1 %collective-permute-done.12.va = f32[4,128,128]{2,1,0:T(8,128)S(1)} collective-permute-done((f32[4,128,128]{2,1,0:T(8,128)S(1)}, f32[4,128,128]{2,1,0:T(8,128)S(1)}, u32[]{:S(2)}, u32[]{:S(2)}) %collective-permute-start.12) | collective-permute-done | bytes 262176 | tf_op jit(solution)/shard_map/ppermute | solution.py:244
  144.9 3.4 %collective-permute-done.11.vb = f32[4,128,128]{2,1,0:T(8,128)S(1)} collective-permute-done((f32[4,128,128]{2,1,0:T(8,128)S(1)}, f32[4,128,128]{2,1,0:T(8,128)S(1)}, u32[]{:S(2)}, u32[]{:S(2)}) %collective-permute-start.11) | collective-permute-done | bytes 262176 | tf_op jit(solution)/shard_map/ppermute | solution.py:244
  148.3 3.7 %shard_map.138 = (f32[3,2,1,120,512]{4,3,2,1,0:T(8,128)}, f32[2,3,1,120,512]{4,3,2,1,0:T(8,128)}, bf16[4,480,512]{2,1,0:T(8,128)(2,1)}) custom-call(s32[4,4]{1,0:T(4,128)S(1)} %bitcast.46, bf16[4,480,480]{2,1,0:T(8,128)(2,1)S(1)} %bitcast.39, f32[2,120,512]{2,1,0:T(8,128)S(1)} %get-tuple-element.28.x0, f32[2,120,512]{2,1,0:T(8,128)S(1)} %get-tuple-element.29.x1, ...), custom_call_target="tpu_custom_call" | custom-call | tf_op jit(solution)/shard_map/pallas_call | solution.py:26
  (59 shorter events, 21.8 us)
Async XLA Ops:
  0.6 10.2 %copy-start = (f32[3,2,1,120,512]{4,3,2,1,0:T(8,128)S(1)}, f32[3,2,1,120,512]{4,3,2,1,0:T(8,128)}, u32[]{:S(2)}) copy-start(f32[3,2,1,120,512]{4,3,2,1,0:T(8,128)} %rx.1) | copy-start | bytes 4423684
  2.4 34.5 %all-to-all-start.2 = ((f32[8,32,512]{2,1,0:T(8,128)}), f32[8,32,512]{2,1,0:T(8,128)S(1)}, u32[]{:S(2)}, u32[]{:S(2)}) async-start(f32[8,32,512]{2,1,0:T(8,128)} %broadcast_in_dim.2), calls=%async_computation.2 | async-start | bytes 1048576 | tf_op jit(solution)/shard_map/all_to_all | solution.py:248
  11.9 4.5 %copy-start.13 = (s32[2,2,1,64]{3,2,1,0:T(1,128)S(1)}, s32[2,2,1,64]{3,2,1,0:T(1,128)}, u32[]{:S(2)}) copy-start(s32[2,2,1,64]{3,2,1,0:T(1,128)} %param.18) | copy-start | bytes 3076
  11.9 18.8 %copy-start.11 = (f32[2,2,1,4,120]{4,3,2,1,0:T(4,128)S(1)}, f32[2,2,1,4,120]{4,3,2,1,0:T(4,128)}, u32[]{:S(2)}) copy-start(f32[2,2,1,4,120]{4,3,2,1,0:T(4,128)} %param.13) | copy-start | bytes 23044
  11.9 18.8 %copy-start.12 = (s32[2,2,1,4]{3,2,1,0:T(1,128)S(1)}, s32[2,2,1,4]{3,2,1,0:T(1,128)}, u32[]{:S(2)}) copy-start(s32[2,2,1,4]{3,2,1,0:T(1,128)} %param.14) | copy-start | bytes 196
  11.9 5.8 %collective-permute-start.1 = (f32[2,120,512]{2,1,0:T(8,128)}, f32[2,120,512]{2,1,0:T(8,128)S(1)}, u32[]{:S(2)}, u32[]{:S(2)}) collective-permute-start(f32[2,120,512]{2,1,0:T(8,128)} %get-tuple-element.44), channel_id=1, source_target_pairs={{0,128},{128,0},{1,129},{129,1},{2,130},{130,2},{3,131},{131,3},{4... | collective-permute-start | bytes 1474568 | tf_op jit(solution)/shard_map/ppermute | solution.py:244
  11.9 5.8 %collective-permute-start = (f32[2,120,512]{2,1,0:T(8,128)}, f32[2,120,512]{2,1,0:T(8,128)S(1)}, u32[]{:S(2)}, u32[]{:S(2)}) collective-permute-start(f32[2,120,512]{2,1,0:T(8,128)} %get-tuple-element.45), channel_id=1, source_target_pairs={{0,128},{128,0},{1,129},{129,1},{2,130},{130,2},{3,131},{131,3},{4... | collective-permute-start | bytes 1474568 | tf_op jit(solution)/shard_map/ppermute | solution.py:244
  13.6 13.6 %collective-permute-start.3 = (f32[2,120,512]{2,1,0:T(8,128)}, f32[2,120,512]{2,1,0:T(8,128)}, u32[]{:S(2)}, u32[]{:S(2)}) collective-permute-start(f32[2,120,512]{2,1,0:T(8,128)} %get-tuple-element.42), channel_id=1, source_target_pairs={{0,96},{32,0},{64,32},{96,64},{1,97},{33,1},{65,33},{97,65},{2,98}... | collective-permute-start | bytes 1474568 | tf_op jit(solution)/shard_map/ppermute | solution.py:244
  16.4 14.3 %collective-permute-start.2 = (f32[2,120,512]{2,1,0:T(8,128)}, f32[2,120,512]{2,1,0:T(8,128)}, u32[]{:S(2)}, u32[]{:S(2)}) collective-permute-start(f32[2,120,512]{2,1,0:T(8,128)} %get-tuple-element.43), channel_id=1, source_target_pairs={{0,32},{32,64},{64,96},{96,0},{1,33},{33,65},{65,97},{97,1},{2,34}... | collective-permute-start | bytes 1474568 | tf_op jit(solution)/shard_map/ppermute | solution.py:244
  36.8 20.2 %all-to-all-start = ((f32[4,264,128]{2,1,0:T(8,128)}), f32[4,264,128]{2,1,0:T(8,128)S(1)}, u32[]{:S(2)}, u32[]{:S(2)}) async-start(f32[4,264,128]{2,1,0:T(8,128)} %copy-done.10), calls=%async_computation | async-start | bytes 1081344 | tf_op jit(solution)/shard_map/all_to_all | solution.py:248
  41.8 34.4 %collective-permute-start.6 = (f32[8,2,16,512]{3,2,1,0:T(8,128)S(1)}, f32[8,2,16,512]{3,2,1,0:T(8,128)S(1)}, u32[]{:S(2)}, u32[]{:S(2)}) collective-permute-start(f32[8,2,16,512]{3,2,1,0:T(8,128)S(1)} %bitcast.28), channel_id=1, source_target_pairs={{0,3},{1,0},{2,1},{3,2},{4,7},{5,4},{6,5},{7,6},{8,11},{9,8},{10,9... | collective-permute-start | bytes 1572872 | tf_op jit(solution)/shard_map/ppermute | solution.py:244
  41.8 34.4 %collective-permute-start.5 = (f32[8,2,16,512]{3,2,1,0:T(8,128)S(1)}, f32[8,2,16,512]{3,2,1,0:T(8,128)S(1)}, u32[]{:S(2)}, u32[]{:S(2)}) collective-permute-start(f32[8,2,16,512]{3,2,1,0:T(8,128)S(1)} %bitcast.29), channel_id=1, source_target_pairs={{0,2},{1,3},{2,0},{3,1},{4,6},{5,7},{6,4},{7,5},{8,10},{9,11},{10,... | collective-permute-start | bytes 1572872 | tf_op jit(solution)/shard_map/ppermute | solution.py:244
  44.7 31.5 %collective-permute-start.4 = (f32[8,2,16,512]{3,2,1,0:T(8,128)S(1)}, f32[8,2,16,512]{3,2,1,0:T(8,128)S(1)}, u32[]{:S(2)}, u32[]{:S(2)}) collective-permute-start(f32[8,2,16,512]{3,2,1,0:T(8,128)S(1)} %bitcast.30), channel_id=1, source_target_pairs={{0,1},{1,2},{2,3},{3,0},{4,5},{5,6},{6,7},{7,4},{8,9},{9,10},{10,1... | collective-permute-start | bytes 1572872 | tf_op jit(solution)/shard_map/ppermute | solution.py:244
  58.5 17.7 %all-to-all-start.1 = ((f32[8,16,512]{2,1,0:T(8,128)}), f32[8,16,512]{2,1,0:T(8,128)S(1)}, u32[]{:S(2)}, u32[]{:S(2)}) async-start(f32[8,16,512]{2,1,0:T(8,128)} %get-tuple-element.24), calls=%async_computation.1 | async-start | bytes 524288 | tf_op jit(solution)/shard_map/all_to_all | solution.py:248
  77.6 10.2 %all-to-all-start.3 = ((f32[8,16,512]{2,1,0:T(8,128)}), f32[8,16,512]{2,1,0:T(8,128)S(1)}, u32[]{:S(2)}, u32[]{:S(2)}) async-start(f32[8,16,512]{2,1,0:T(8,128)} %get-tuple-element.25), calls=%async_computation.3 | async-start | bytes 524288 | tf_op jit(solution)/shard_map/all_to_all | solution.py:248
  91.0 24.8 %copy-start.5 = (bf16[2,2,1,480,480]{4,3,2,1,0:T(8,128)(2,1)S(1)}, bf16[2,2,1,480,480]{4,3,2,1,0:T(8,128)(2,1)}, u32[]{:S(2)}) copy-start(bf16[2,2,1,480,480]{4,3,2,1,0:T(8,128)(2,1)} %param.15) | copy-start | bytes 5529604
  107.6 18.6 %all-to-all-start.5 = ((f32[4,256,128]{2,1,0:T(8,128)}), f32[4,256,128]{2,1,0:T(8,128)S(1)}, u32[]{:S(2)}, u32[]{:S(2)}) async-start(f32[4,256,128]{2,1,0:T(8,128)} %shard_map.136), calls=%async_computation.5 | async-start | bytes 1048576 | tf_op jit(solution)/shard_map/all_to_all | solution.py:248
  123.0 17.0 %collective-permute-start.9 = (f32[2,120,640]{2,1,0:T(8,128)}, f32[2,120,640]{2,1,0:T(8,128)S(1)}, u32[]{:S(2)}, u32[]{:S(2)}) collective-permute-start(f32[2,120,640]{2,1,0:T(8,128)} %get-tuple-element.34), channel_id=1, source_target_pairs={{0,32},{32,64},{64,96},{96,0},{1,33},{33,65},{65,97},{97,1},{2,34}... | collective-permute-start | bytes 1843208 | tf_op jit(solution)/shard_map/ppermute | solution.py:244
  123.9 16.9 %collective-permute-start.10 = (f32[2,120,640]{2,1,0:T(8,128)}, f32[2,120,640]{2,1,0:T(8,128)S(1)}, u32[]{:S(2)}, u32[]{:S(2)}) collective-permute-start(f32[2,120,640]{2,1,0:T(8,128)} %get-tuple-element.35), channel_id=1, source_target_pairs={{0,96},{32,0},{64,32},{96,64},{1,97},{33,1},{65,33},{97,65},{2,98}... | collective-permute-start | bytes 1843208 | tf_op jit(solution)/shard_map/ppermute | solution.py:244
  128.3 19.9 %copy-start.6 = (bf16[2,2,1,480,480]{4,3,2,1,0:T(8,128)(2,1)S(1)}, bf16[2,2,1,480,480]{4,3,2,1,0:T(8,128)(2,1)}, u32[]{:S(2)}) copy-start(bf16[2,2,1,480,480]{4,3,2,1,0:T(8,128)(2,1)} %param.16) | copy-start | bytes 5529604
  130.3 17.9 %collective-permute-start.8 = (f32[2,120,512]{2,1,0:T(8,128)S(1)}, f32[2,120,512]{2,1,0:T(8,128)S(1)}, u32[]{:S(2)}, u32[]{:S(2)}) collective-permute-start(f32[2,120,512]{2,1,0:T(8,128)S(1)} %get-tuple-element.28.x0), channel_id=1, source_target_pairs={{0,128},{128,0},{1,129},{129,1},{2,130},{130,2},{3,131},{131,3},{4... | collective-permute-start | bytes 1474568 | tf_op jit(solution)/shard_map/ppermute | solution.py:244
  130.4 17.8 %collective-permute-start.7 = (f32[2,120,512]{2,1,0:T(8,128)S(1)}, f32[2,120,512]{2,1,0:T(8,128)S(1)}, u32[]{:S(2)}, u32[]{:S(2)}) collective-permute-start(f32[2,120,512]{2,1,0:T(8,128)S(1)} %get-tuple-element.30.x2), channel_id=1, source_target_pairs={{0,128},{128,0},{1,129},{129,1},{2,130},{130,2},{3,131},{131,3},{4... | collective-permute-start | bytes 1474568 | tf_op jit(solution)/shard_map/ppermute | solution.py:244
  131.0 13.9 %collective-permute-start.12 = (f32[4,128,128]{2,1,0:T(8,128)S(1)}, f32[4,128,128]{2,1,0:T(8,128)S(1)}, u32[]{:S(2)}, u32[]{:S(2)}) collective-permute-start(f32[4,128,128]{2,1,0:T(8,128)S(1)} %get-tuple-element.46), channel_id=1, source_target_pairs={{0,96},{32,0},{64,32},{96,64},{1,97},{33,1},{65,33},{97,65},{2,98}... | collective-permute-start | bytes 786440 | tf_op jit(solution)/shard_map/ppermute | solution.py:244
  139.9 8.3 %collective-permute-start.11 = (f32[4,128,128]{2,1,0:T(8,128)S(1)}, f32[4,128,128]{2,1,0:T(8,128)S(1)}, u32[]{:S(2)}, u32[]{:S(2)}) collective-permute-start(f32[4,128,128]{2,1,0:T(8,128)S(1)} %get-tuple-element.47), channel_id=1, source_target_pairs={{0,32},{32,64},{64,96},{96,0},{1,33},{33,65},{65,97},{97,1},{2,34}... | collective-permute-start | bytes 786440 | tf_op jit(solution)/shard_map/ppermute | solution.py:244
  (8 other events, 11.9 us)
